TPU v7x, 32 devices: a whole 2x2x4 slice. The times are simulated.
32 devices in a mesh: seq: 8 (over y, x, core), fsdp: 4 (over z).
Axes of the slice: x: 2, y: 2, z: 4, core: 2. Of those that a mesh axis runs over, the one named last changes fastest.
Arguments:
- normed: bfloat16 [32768, 1024], P(('seq', 'fsdp')), may hold values from -31 to 31, as said below
- w_qkv: bfloat16 [1024, 3072], P('fsdp'), may hold values from -0.5 to 0.5, as said below
- w_out: bfloat16 [1024, 1024], P('fsdp'), may hold values from -0.5 to 0.5
- layout: int32 [256, 10], P(('seq', 'fsdp')), may hold values from 0 to 23, as said below
- counts: int32 [256], P(('seq', 'fsdp')), may hold values from 1 to 10, as said below
Outputs:
- mixed: bfloat16 [32768, 1024], P(('seq', 'fsdp'))
Inputs may be any that keep to these rules, and one draw needn't show every extreme that they name: `normed`: float activations. `w_qkv`: float weights. `layout`: each row holds 10 distinct pool entries, never the query block's own entry; entries 0 to 7 name the blocks of the station one step lower along seq, the last 8 those one step higher. `counts`: the value 10 occurs in every draw.
All inputs are finite; a program needn't handle non-finite values.
Results may differ from a plain program's by a relative error of at most 0.0099.
Values may be sent and summed in bfloat16 or wider, within the bound.
No kernel may reach another device: no remote copies, remote signals or barrier semaphores. Data moves between devices by JAX's collectives and lax.ppermute only.
A program may use at most 128 MiB of HBM per device.

v0:
```python
import math
import jax
import jax.numpy as jnp
from jax import lax
from jax.sharding import PartitionSpec as P

HEADS = 8
BLOCK = 128
KEY_BLOCKS = 10


def from_behind(value, axis, steps):
    count = lax.axis_size(axis)
    pairs = [(source, (source + steps) % count) for source in range(count)]
    return lax.ppermute(value, axis, pairs)


def attend(query, own_blocks, picked, used):
    block_count = picked.shape[0]
    feature_width = query.shape[1]
    head_width = feature_width // HEADS
    keyvals = jnp.concatenate([own_blocks[:, None], picked], axis=1)
    keyvals = keyvals.reshape(block_count, (KEY_BLOCKS + 1) * BLOCK, 2 * feature_width)
    key_heads = keyvals[..., :feature_width].reshape(block_count, -1, HEADS, head_width)
    value_heads = keyvals[..., feature_width:].reshape(block_count, -1, HEADS, head_width)
    query_heads = query.reshape(block_count, BLOCK, HEADS, head_width)
    scores = jnp.einsum(
        "bqhd,bkhd->bhqk", query_heads, key_heads, preferred_element_type=jnp.float32
    )
    scores = scores * head_width ** (-0.5)
    slot_number = jnp.arange((KEY_BLOCKS + 1) * BLOCK, dtype=jnp.int32) // BLOCK
    usable = slot_number[None, :] <= used[:, None]
    scores = jnp.where(usable[:, None, None, :], scores, -jnp.inf)
    largest = jnp.max(scores, axis=-1, keepdims=True)
    expons = jnp.exp(scores - largest)
    denominator = jnp.sum(expons, axis=-1, keepdims=True)
    rounded = expons.astype(jnp.bfloat16)
    summed = jnp.einsum("bhqk,bkhd->bqhd", rounded, value_heads, preferred_element_type=jnp.float32)
    summed = summed / jnp.transpose(denominator, (0, 2, 1, 3))
    return summed.reshape(block_count * BLOCK, feature_width).astype(jnp.bfloat16)


def shards(normed, w_qkv, w_out, layout, counts):
    row_count, feature_width = normed.shape
    blocks_here = row_count // BLOCK
    lower_tokens = from_behind(normed, "seq", 1)
    upper_tokens = from_behind(normed, "seq", -1)
    sources = (normed, lower_tokens, upper_tokens)
    start_sums = [jnp.zeros((row_count, 3 * feature_width), jnp.float32)]
    for member in range(1, len(sources)):
        start_sums.append(jnp.zeros((row_count, 2 * feature_width), jnp.float32))
    start_sums = tuple(start_sums)
    weight_rows = lax.all_gather(w_qkv, "fsdp", axis=0, tiled=True)
    own_cols = sources[0]
    fresh = [jnp.dot(own_cols, weight_rows, preferred_element_type=jnp.float32)]
    for member in range(1, len(sources)):
        side_cols = sources[member]
        fresh.append(
            jnp.dot(side_cols, weight_rows[:, feature_width:], preferred_element_type=jnp.float32)
        )
    sums = tuple(fresh)
    packed = sums[0].astype(jnp.bfloat16)
    queries = packed[:, :feature_width]
    keyvals = packed[:, feature_width:]
    pool_rows = jnp.concatenate(
        [sums[1].astype(jnp.bfloat16), keyvals, sums[2].astype(jnp.bfloat16)], axis=0
    )
    pool = pool_rows.reshape(3 * blocks_here, BLOCK, 2 * feature_width)
    group_size = math.gcd(blocks_here, max(1, 256 // BLOCK))
    group_count = blocks_here // group_size

    def one_group(items):
        query_part, layout_part, count_part, group_number = items
        own_blocks = lax.dynamic_slice_in_dim(
            pool, blocks_here + group_number * group_size, group_size, 0
        )
        picked = pool[layout_part]
        return attend(query_part, own_blocks, picked, count_part)

    attended = lax.map(
        one_group,
        (
            queries.reshape(group_count, group_size * BLOCK, feature_width),
            layout.reshape(group_count, group_size, KEY_BLOCKS),
            counts.reshape(group_count, group_size),
            jnp.arange(group_count, dtype=jnp.int32),
        ),
    )
    attended = attended.reshape(row_count, feature_width)
    output_sum = jnp.dot(
        attended,
        lax.all_gather(w_out, "fsdp", axis=0, tiled=True),
        preferred_element_type=jnp.float32,
    )
    return output_sum.astype(jnp.bfloat16)


def solution(mesh):
    return jax.shard_map(
        shards,
        mesh=mesh,
        in_specs=(
            P(("seq", "fsdp"), None),
            P("fsdp", None),
            P("fsdp", None),
            P(("seq", "fsdp"), None),
            P(("seq", "fsdp")),
        ),
        out_specs=P(("seq", "fsdp"), None),
        check_vma=False,
    )
```

profile of v0, /device:TPU:0, one launch (start us, length us, event | category | flops | bytes accessed | tf_op | source)
XLA Modules:
  0.0 460.4 jit_solution(16126469676680698676)
XLA Ops:
  6.5 0.7 all-gather.3.cloned.1.call-update
  7.3 3.4 collective-permute-start.1
  10.8 0.7 reshape.143
  11.5 115.5 %all-gather.3.cloned.1.call-done = bf16[1024,3072]{1,0:T(8,128)(2,1)} async-done(((bf16[256,3072]{1,0:T(8,128)(2,1)}), bf16[1024,3072]{1,0:T(8,128)(2,1)}) %all-gather.3.cloned.1.call-update) | async-done | bytes 6291472 | tf_op jit(solution)/shard_map/all_gather | solution.py:53
  127.0 9.4 %convolution_convert_fusion = bf16[1024,3072]{1,0:T(8,128)(2,1)S(1)} fusion(bf16[1024,1024]{1,0:T(8,128)(2,1)} %param.7, bf16[1024,3072]{1,0:T(8,128)(2,1)} %all-gather.3.cloned.1.call-done), kind=kOutput, calls=%fused_computation.36 | convolution fusion | flops 6445596672 | bytes 14680064 | tf_op jit(solution)/shard_map/dot_general | solution.py:55
  136.4 3.2 copy-done.1
  139.6 1.9 copy-done.2
  141.5 6.3 %convolution_convert_fusion.1 = bf16[1024,2048]{1,0:T(8,128)(2,1)S(1)} fusion(bf16[1024,1024]{1,0:T(8,128)(2,1)} %collective-permute-done.1, bf16[1024,3072]{1,0:T(8,128)(2,1)S(1)} %copy-done.2), kind=kOutput, calls=%fused_computation.37 | convolution fusion | flops 4297064448 | bytes 10485760 | tf_op jit(solution)/shard_map/dot_general | solution.py:59
  147.8 4.7 %convolution_convert_fusion.2 = bf16[1024,2048]{1,0:T(8,128)(2,1)S(1)} fusion(bf16[1024,1024]{1,0:T(8,128)(2,1)S(1)} %collective-permute-done, bf16[1024,3072]{1,0:T(8,128)(2,1)S(1)} %copy-done.2), kind=kOutput, calls=%fused_computation.38 | convolution fusion | flops 4297064448 | bytes 10485760 | tf_op jit(solution)/shard_map/dot_general | solution.py:59
  152.6 21.3 %pad_maximum_fusion.1 = bf16[3072,2048]{1,0:T(8,128)(2,1)} fusion(bf16[1024,2048]{1,0:T(8,128)(2,1)S(1)} %convolution_convert_fusion.1, bf16[1024,2048]{1,0:T(8,128)(2,1)S(1)} %slice-done, bf16[1024,2048]{1,0:T(8,128)(2,1)S(1)} %convolution_convert_fusion.2), kind=kLoop, calls=%fused_computation.35 | loop fusion | flops 37748736 | bytes 25165824 | tf_op jit(solution)/shard_map/concatenate | solution.py:65
  173.9 273.7 %while.12 = (s32[]{:T(128)}, bf16[4,256,1024]{2,1,0:T(8,128)(2,1)}, s32[4]{0:T(128)S(1)}, bf16[24,128,2048]{2,1,0:T(8,128)(2,1)}, s32[4,2,10]{2,1,0:T(2,128)}, /...) while((s32[]{:T(128)}, bf16[4,256,1024]{2,1,0:T(8,128)(2,1)}, ...), condition=%wide.region_3.4_spmd, body=%wide.region_0.3_spmd.sunk | while | flops 1514416896 | bytes 190909680 | solution.py:80
  173.9 0.6 dynamic_slice.53
  175.2 1.3 dynamic-slice_bitcast_fusion.4
  176.5 0.7 compare_select_fusion.2
  177.3 10.0 %gather_fusion = bf16[20,128,2048]{2,1,0:T(8,128)(2,1)} fusion(bf16[24,128,2048]{2,1,0:T(8,128)(2,1)} %get-tuple-element.200, s32[1024]{0:T(1024)S(1)} %pad_clamp_fusion.2), kind=kCustom, calls=%fused_computation.clone.1 | custom fusion | bytes 20971600 | tf_op jit(solution)/shard_map/while/body/eval_jaxpr/gather | solution.py:77
  187.3 10.1 %pad_maximum_fusion.3 = bf16[2,11,128,2048]{3,2,1,0:T(8,128)(2,1)} fusion(bf16[2,10,128,2048]{3,2,1,0:T(8,128)(2,1)} %bitcast.76, bf16[2,1,128,2048]{3,2,1,0:T(8,128)(2,1)S(1)} %dynamic-slice_bitcast_fusion.4), kind=kLoop, calls=%fused_computation.1.clone.1 | loop fusion | flops 5767168 | bytes 23068672 | tf_op jit(solution)/shard_map/while/body/eval_jaxpr/concatenate | solution.py:22
  197.3 9.9 %fusion.44 = (bf16[2,1408,1024]{2,1,0:T(8,128)(2,1)}, bf16[2,1408,1024]{2,1,0:T(8,128)(2,1)}) fusion(bf16[2,1408,2048]{2,1,0:T(8,128)(2,1)} %bitcast.74), kind=kLoop, calls=%fused_computation.42.clone.1 | loop fusion | bytes 23068672 | tf_op jit(solution)/shard_map/while/body/eval_jaxpr/slice | solution.py:24
  207.3 8.2 %copy.26 = bf16[2,1408,1024]{1,2,0:T(8,128)(2,1)} copy(bf16[2,1408,1024]{2,1,0:T(8,128)(2,1)} %get-tuple-element.170) | data formatting | bytes 11534336 | tf_op jit(solution)/shard_map/while/body/eval_jaxpr/slice | solution.py:24
  215.7 3.9 fusion.46
  219.6 2.4 fusion.47
  222.1 1.8 copy-done
  223.8 8.3 %copy.25 = bf16[2,1408,1024]{1,2,0:T(8,128)(2,1)} copy(bf16[2,1408,1024]{2,1,0:T(8,128)(2,1)} %get-tuple-element.169) | data formatting | bytes 11534336 | tf_op jit(solution)/shard_map/while/body/eval_jaxpr/slice | solution.py:25
  232.2 8.8 %divide_convert_fusion.2 = bf16[2,128,8,128]{1,3,2,0:T(8,128)(2,1)S(1)} fusion(bf16[2,1408,8,128]{1,3,2,0:T(8,128)(2,1)} %bitcast.78, f32[2,8,128,1408]{3,2,1,0:T(8,128)} %copy-done, f32[2,8,128]{2,1,0:T(8,128)S(1)} %get-tuple-element.172, pred[2,1408]{1,0:T(4,128)(4,1)S(1)} %broadcast_compare_fusion.2, f32[2,128,8]{1,2,0:T(8,128)S(1)} %bitcast.81), kind=kOutput, calls=%fused_computation.13.clone.1 | convolution fusion | flops 750256128 | bytes 17844992 | tf_op jit(solution)/shard_map/while/body/eval_jaxpr/bhqk,bkhd->bqhd/dot_general | solution.py:38
  241.5 0.8 constant_dynamic-update-slice_fusion.2
  242.3 0.6 dynamic_slice.53
  243.6 1.3 dynamic-slice_bitcast_fusion.4
  244.9 0.7 compare_select_fusion.2
  245.7 10.0 %gather_fusion = bf16[20,128,2048]{2,1,0:T(8,128)(2,1)} fusion(bf16[24,128,2048]{2,1,0:T(8,128)(2,1)} %get-tuple-element.200, s32[1024]{0:T(1024)S(1)} %pad_clamp_fusion.2), kind=kCustom, calls=%fused_computation.clone.1 | custom fusion | bytes 20971600 | tf_op jit(solution)/shard_map/while/body/eval_jaxpr/gather | solution.py:77
  255.7 10.1 %pad_maximum_fusion.3 = bf16[2,11,128,2048]{3,2,1,0:T(8,128)(2,1)} fusion(bf16[2,10,128,2048]{3,2,1,0:T(8,128)(2,1)} %bitcast.76, bf16[2,1,128,2048]{3,2,1,0:T(8,128)(2,1)S(1)} %dynamic-slice_bitcast_fusion.4), kind=kLoop, calls=%fused_computation.1.clone.1 | loop fusion | flops 5767168 | bytes 23068672 | tf_op jit(solution)/shard_map/while/body/eval_jaxpr/concatenate | solution.py:22
  265.8 9.9 %fusion.44 = (bf16[2,1408,1024]{2,1,0:T(8,128)(2,1)}, bf16[2,1408,1024]{2,1,0:T(8,128)(2,1)}) fusion(bf16[2,1408,2048]{2,1,0:T(8,128)(2,1)} %bitcast.74), kind=kLoop, calls=%fused_computation.42.clone.1 | loop fusion | bytes 23068672 | tf_op jit(solution)/shard_map/while/body/eval_jaxpr/slice | solution.py:24
  275.7 8.2 %copy.26 = bf16[2,1408,1024]{1,2,0:T(8,128)(2,1)} copy(bf16[2,1408,1024]{2,1,0:T(8,128)(2,1)} %get-tuple-element.170) | data formatting | bytes 11534336 | tf_op jit(solution)/shard_map/while/body/eval_jaxpr/slice | solution.py:24
  284.2 3.9 fusion.46
  288.1 2.4 fusion.47
  290.5 1.8 copy-done
  292.2 8.3 %copy.25 = bf16[2,1408,1024]{1,2,0:T(8,128)(2,1)} copy(bf16[2,1408,1024]{2,1,0:T(8,128)(2,1)} %get-tuple-element.169) | data formatting | bytes 11534336 | tf_op jit(solution)/shard_map/while/body/eval_jaxpr/slice | solution.py:25
  300.6 8.8 %divide_convert_fusion.2 = bf16[2,128,8,128]{1,3,2,0:T(8,128)(2,1)S(1)} fusion(bf16[2,1408,8,128]{1,3,2,0:T(8,128)(2,1)} %bitcast.78, f32[2,8,128,1408]{3,2,1,0:T(8,128)} %copy-done, f32[2,8,128]{2,1,0:T(8,128)S(1)} %get-tuple-element.172, pred[2,1408]{1,0:T(4,128)(4,1)S(1)} %broadcast_compare_fusion.2, f32[2,128,8]{1,2,0:T(8,128)S(1)} %bitcast.81), kind=kOutput, calls=%fused_computation.13.clone.1 | convolution fusion | flops 750256128 | bytes 17844992 | tf_op jit(solution)/shard_map/while/body/eval_jaxpr/bhqk,bkhd->bqhd/dot_general | solution.py:38
  309.9 0.9 constant_dynamic-update-slice_fusion.2
  310.8 0.6 dynamic_slice.53
  312.1 1.3 dynamic-slice_bitcast_fusion.4
  313.4 0.7 compare_select_fusion.2
  314.1 10.0 %gather_fusion = bf16[20,128,2048]{2,1,0:T(8,128)(2,1)} fusion(bf16[24,128,2048]{2,1,0:T(8,128)(2,1)} %get-tuple-element.200, s32[1024]{0:T(1024)S(1)} %pad_clamp_fusion.2), kind=kCustom, calls=%fused_computation.clone.1 | custom fusion | bytes 20971600 | tf_op jit(solution)/shard_map/while/body/eval_jaxpr/gather | solution.py:77
  324.1 10.1 %pad_maximum_fusion.3 = bf16[2,11,128,2048]{3,2,1,0:T(8,128)(2,1)} fusion(bf16[2,10,128,2048]{3,2,1,0:T(8,128)(2,1)} %bitcast.76, bf16[2,1,128,2048]{3,2,1,0:T(8,128)(2,1)S(1)} %dynamic-slice_bitcast_fusion.4), kind=kLoop, calls=%fused_computation.1.clone.1 | loop fusion | flops 5767168 | bytes 23068672 | tf_op jit(solution)/shard_map/while/body/eval_jaxpr/concatenate | solution.py:22
  334.2 9.9 %fusion.44 = (bf16[2,1408,1024]{2,1,0:T(8,128)(2,1)}, bf16[2,1408,1024]{2,1,0:T(8,128)(2,1)}) fusion(bf16[2,1408,2048]{2,1,0:T(8,128)(2,1)} %bitcast.74), kind=kLoop, calls=%fused_computation.42.clone.1 | loop fusion | bytes 23068672 | tf_op jit(solution)/shard_map/while/body/eval_jaxpr/slice | solution.py:24
  344.2 8.2 %copy.26 = bf16[2,1408,1024]{1,2,0:T(8,128)(2,1)} copy(bf16[2,1408,1024]{2,1,0:T(8,128)(2,1)} %get-tuple-element.170) | data formatting | bytes 11534336 | tf_op jit(solution)/shard_map/while/body/eval_jaxpr/slice | solution.py:24
  352.6 3.9 fusion.46
  356.5 2.4 fusion.47
  358.9 1.8 copy-done
  360.7 8.3 %copy.25 = bf16[2,1408,1024]{1,2,0:T(8,128)(2,1)} copy(bf16[2,1408,1024]{2,1,0:T(8,128)(2,1)} %get-tuple-element.169) | data formatting | bytes 11534336 | tf_op jit(solution)/shard_map/while/body/eval_jaxpr/slice | solution.py:25
  369.0 8.8 %divide_convert_fusion.2 = bf16[2,128,8,128]{1,3,2,0:T(8,128)(2,1)S(1)} fusion(bf16[2,1408,8,128]{1,3,2,0:T(8,128)(2,1)} %bitcast.78, f32[2,8,128,1408]{3,2,1,0:T(8,128)} %copy-done, f32[2,8,128]{2,1,0:T(8,128)S(1)} %get-tuple-element.172, pred[2,1408]{1,0:T(4,128)(4,1)S(1)} %broadcast_compare_fusion.2, f32[2,128,8]{1,2,0:T(8,128)S(1)} %bitcast.81), kind=kOutput, calls=%fused_computation.13.clone.1 | convolution fusion | flops 750256128 | bytes 17844992 | tf_op jit(solution)/shard_map/while/body/eval_jaxpr/bhqk,bkhd->bqhd/dot_general | solution.py:38
  378.4 0.8 constant_dynamic-update-slice_fusion.2
  379.2 0.6 dynamic_slice.53
  380.5 1.3 dynamic-slice_bitcast_fusion.4
  381.8 0.7 compare_select_fusion.2
  382.6 10.0 %gather_fusion = bf16[20,128,2048]{2,1,0:T(8,128)(2,1)} fusion(bf16[24,128,2048]{2,1,0:T(8,128)(2,1)} %get-tuple-element.200, s32[1024]{0:T(1024)S(1)} %pad_clamp_fusion.2), kind=kCustom, calls=%fused_computation.clone.1 | custom fusion | bytes 20971600 | tf_op jit(solution)/shard_map/while/body/eval_jaxpr/gather | solution.py:77
  392.6 10.1 %pad_maximum_fusion.3 = bf16[2,11,128,2048]{3,2,1,0:T(8,128)(2,1)} fusion(bf16[2,10,128,2048]{3,2,1,0:T(8,128)(2,1)} %bitcast.76, bf16[2,1,128,2048]{3,2,1,0:T(8,128)(2,1)S(1)} %dynamic-slice_bitcast_fusion.4), kind=kLoop, calls=%fused_computation.1.clone.1 | loop fusion | flops 5767168 | bytes 23068672 | tf_op jit(solution)/shard_map/while/body/eval_jaxpr/concatenate | solution.py:22
  402.7 9.9 %fusion.44 = (bf16[2,1408,1024]{2,1,0:T(8,128)(2,1)}, bf16[2,1408,1024]{2,1,0:T(8,128)(2,1)}) fusion(bf16[2,1408,2048]{2,1,0:T(8,128)(2,1)} %bitcast.74), kind=kLoop, calls=%fused_computation.42.clone.1 | loop fusion | bytes 23068672 | tf_op jit(solution)/shard_map/while/body/eval_jaxpr/slice | solution.py:24
  412.6 8.2 %copy.26 = bf16[2,1408,1024]{1,2,0:T(8,128)(2,1)} copy(bf16[2,1408,1024]{2,1,0:T(8,128)(2,1)} %get-tuple-element.170) | data formatting | bytes 11534336 | tf_op jit(solution)/shard_map/while/body/eval_jaxpr/slice | solution.py:24
  421.1 3.9 fusion.46
  424.9 2.4 fusion.47
  427.4 1.8 copy-done
  429.1 8.3 %copy.25 = bf16[2,1408,1024]{1,2,0:T(8,128)(2,1)} copy(bf16[2,1408,1024]{2,1,0:T(8,128)(2,1)} %get-tuple-element.169) | data formatting | bytes 11534336 | tf_op jit(solution)/shard_map/while/body/eval_jaxpr/slice | solution.py:25
  437.5 8.8 %divide_convert_fusion.2 = bf16[2,128,8,128]{1,3,2,0:T(8,128)(2,1)S(1)} fusion(bf16[2,1408,8,128]{1,3,2,0:T(8,128)(2,1)} %bitcast.78, f32[2,8,128,1408]{3,2,1,0:T(8,128)} %copy-done, f32[2,8,128]{2,1,0:T(8,128)S(1)} %get-tuple-element.172, pred[2,1408]{1,0:T(4,128)(4,1)S(1)} %broadcast_compare_fusion.2, f32[2,128,8]{1,2,0:T(8,128)S(1)} %bitcast.81), kind=kOutput, calls=%fused_computation.13.clone.1 | convolution fusion | flops 750256128 | bytes 17844992 | tf_op jit(solution)/shard_map/while/body/eval_jaxpr/bhqk,bkhd->bqhd/dot_general | solution.py:38
  446.8 0.8 constant_dynamic-update-slice_fusion.2
  447.6 5.9 %convolution_convert_fusion.3 = bf16[1024,1024]{1,0:T(8,128)(2,1)} fusion(bf16[1024,1024]{1,0:T(8,128)(2,1)} %bitcast.83, bf16[1024,1024]{1,0:T(8,128)(2,1)} %all-gather.5.cloned.1.call-done), kind=kOutput, calls=%fused_computation.41 | convolution fusion | flops 2148532224 | bytes 6291456 | tf_op jit(solution)/shard_map/dot_general | solution.py:90
  (55 shorter events, 3.4 us)
Async XLA Ops:
  6.5 120.5 %all-gather.3.cloned.1.call-start = ((), (), s32[]{:S(2)}) async-start(), calls=%async_computation | async-start | bytes 7864320 | tf_op jit(solution)/shard_map/all_gather | solution.py:53
  7.3 440.4 %all-gather.5.cloned.1.call-start = ((), (), s32[]{:S(2)}) async-start(), calls=%async_computation.1 | async-start | bytes 2621440 | tf_op jit(solution)/shard_map/all_gather | solution.py:92
  7.3 132.3 %collective-permute-start.1 = (bf16[1024,1024]{1,0:T(8,128)(2,1)}, bf16[1024,1024]{1,0:T(8,128)(2,1)}, u32[]{:S(2)}, u32[]{:S(2)}) collective-permute-start(bf16[1024,1024]{1,0:T(8,128)(2,1)} %param.7), channel_id=1, source_target_pairs={{0,28},{4,0},{8,4},{12,8},{16,12},{20,16},{24,20},{28,24},{1,29},{... | collective-permute-start | bytes 6291464 | tf_op jit(solution)/shard_map/ppermute | solution.py:15
  10.7 137.1 %collective-permute-start = (bf16[1024,1024]{1,0:T(8,128)(2,1)}, bf16[1024,1024]{1,0:T(8,128)(2,1)S(1)}, u32[]{:S(2)}, u32[]{:S(2)}) collective-permute-start(bf16[1024,1024]{1,0:T(8,128)(2,1)} %param.7), channel_id=1, source_target_pairs={{0,4},{4,8},{8,12},{12,16},{16,20},{20,24},{24,28},{28,0},{1,5},{5... | collective-permute-start | bytes 6291464 | tf_op jit(solution)/shard_map/ppermute | solution.py:15
  136.4 3.2 copy-start.1
  136.4 5.1 %copy-start.2 = (bf16[1024,3072]{1,0:T(8,128)(2,1)S(1)}, bf16[1024,3072]{1,0:T(8,128)(2,1)}, u32[]{:S(2)}) copy-start(bf16[1024,3072]{1,0:T(8,128)(2,1)} %all-gather.3.cloned.1.call-done) | copy-start | bytes 18874372
  147.8 4.8 %slice-start = ((bf16[1024,3072]{1,0:T(8,128)(2,1)}), bf16[1024,2048]{1,0:T(8,128)(2,1)S(1)}, s32[]{:S(2)}) async-start(bf16[1024,3072]{1,0:T(8,128)(2,1)} %copy-done.1), calls=%async_computation.2 | async-start | bytes 8388608 | tf_op jit(solution)/shard_map/slice | solution.py:64
  152.6 21.3 %slice-start.1 = ((bf16[1024,3072]{1,0:T(8,128)(2,1)}), bf16[1024,1024]{1,0:T(8,128)(2,1)S(1)}, s32[]{:S(2)}) async-start(bf16[1024,3072]{1,0:T(8,128)(2,1)} %copy-done.1), calls=%async_computation.3 | async-start | bytes 4194304 | tf_op jit(solution)/shard_map/slice | solution.py:63
  219.6 4.2 copy-start
  288.1 4.2 copy-start
  356.5 4.2 copy-start
  424.9 4.2 copy-start
Sparse Core Ops, SparseCore 0:
  8.9 118.0 all-gather.2
  128.6 43.8 all-gather.4
where the time goes:
time: 463 us; the launch traced here: 460 us
  local copies, waits for them, and re-layouts  173 us (37%)
  waiting for transfers between devices  116 us (25%)
  matrix products  77.1 us (17%)
  other arithmetic  74.4 us (16%)
  between operations  13.5 us (3%)
    all_gather x1, waiting for transfers between devices, shards(): weight_rows = lax.all_gather(w_qkv, 'fsdp', axis=0, tiled=True)  115 us
    slice x8, local copies, waits for them, and re-layouts, attend(): keyvals[..., :feature_width].reshape(block_count, -1, HEADS, head_width)  72.7 us
    concatenate x4, other arithmetic, attend(): keyvals = jnp.concatenate([own_blocks[:, None], picked], axis=1)  40.3 us
    gather x4, local copies, waits for them, and re-layouts, one_group(): picked = pool[layout_part]  40 us
    dot_general x4, matrix products, attend(): jnp.einsum('bhqk,bkhd->bqhd', rounded, value_heads, preferred_element_typ...  35.2 us
    slice x4, local copies, waits for them, and re-layouts, attend(): keyvals[..., feature_width:].reshape(block_count, -1, HEADS, head_width)  33.3 us
    concatenate x1, other arithmetic, shards(): jnp.concatenate([sums[1].astype(jnp.bfloat16), keyvals, sums[2].astype(jn...  21.3 us
    dot_general x4, matrix products, attend(): jnp.einsum('bqhd,bkhd->bhqk', query_heads, key_heads, preferred_element_t...  15.5 us
  transfers between devices with their start and end apart: 4, of which 1 were waited for; matrix products, arithmetic and copies ran while one was open for 67% of the time, Pallas kernels for 0%

commit v1 on v0

--- a/solution.py
+++ b/solution.py
@@ -7,6 +7,28 @@
 HEADS = 8
 BLOCK = 128
 KEY_BLOCKS = 10
+
+
+def in_order(blocks, dim):
+    blocks = jnp.moveaxis(blocks, 0, dim)
+    lengths = blocks.shape
+    return blocks.reshape(*lengths[:dim], lengths[dim] * lengths[dim + 1], *lengths[dim + 2 :])
+
+
+def ring_gather(x, axis, dim):
+    peers = lax.axis_size(axis)
+    pairs = [(i, (i + 1) % peers) for i in range(peers)]
+    back = [(b, a) for a, b in pairs]
+    lower, upper = ([], [])
+    for step in range(peers - 1):
+        if step % 2 == 0:
+            lower.append(lax.ppermute(lower[-1] if lower else x, axis, pairs))
+        else:
+            upper.append(lax.ppermute(upper[-1] if upper else x, axis, back))
+    blocks = jnp.stack([*lower[::-1], x, *upper])
+    shift = lax.axis_index(axis) - len(lower)
+    blocks = blocks[(jnp.arange(peers) - shift) % peers]
+    return in_order(blocks, dim)
 
 
 def from_behind(value, axis, steps):
@@ -50,7 +72,7 @@
     for member in range(1, len(sources)):
         start_sums.append(jnp.zeros((row_count, 2 * feature_width), jnp.float32))
     start_sums = tuple(start_sums)
-    weight_rows = lax.all_gather(w_qkv, "fsdp", axis=0, tiled=True)
+    weight_rows = ring_gather(w_qkv, "fsdp", 0)
     own_cols = sources[0]
     fresh = [jnp.dot(own_cols, weight_rows, preferred_element_type=jnp.float32)]
     for member in range(1, len(sources)):

time: 463 us -> 503 us (1.086); the launches traced: 460 us -> 495 us
  local copies, waits for them, and re-layouts: 173 us -> 189 us
  waiting for transfers between devices: 116 us -> 125 us
  other arithmetic: 74.4 us -> 79.7 us
    ppermute x0 -> x3, waiting for transfers between devices: none -> 125 us  [the longest x2 93.8 us: ring_gather(): lower.append(lax.ppermute(lower[-1] if lower else x, axis, pairs))]
    all_gather x1 -> x0, waiting for transfers between devices: 115 us -> none  [shards(): weight_rows = lax.all_gather(w_qkv, 'fsdp', axis=0, tiled=True)]
    while x16, local copies, waits for them, and re-layouts: 7.54 us -> 17.2 us
    gather x0 -> x1, local copies, waits for them, and re-layouts: none -> 6.52 us  [ring_gather(): blocks = blocks[(jnp.arange(peers) - shift) % peers]]
    another operation x0 -> x1, other arithmetic: none -> 5.22 us  [ring_gather(): blocks = jnp.stack([*lower[::-1], x, *upper])]
    ppermute x0 -> x3, starting transfers between devices: none -> 5.08 us  [the longest x2 3.05 us: ring_gather(): lower.append(lax.ppermute(lower[-1] if lower else x, axis, pairs))]
  transfers between devices with their start and end apart: 4 -> 6, of which waited for: 1 -> 3; matrix products, arithmetic and copies ran while one was open for 67% -> 65% of each run, Pallas kernels for 0% -> 0%
where the time goes in v1:
time: 503 us; the launch traced here: 495 us
  local copies, waits for them, and re-layouts  189 us (38%)
  waiting for transfers between devices  125 us (25%)
  other arithmetic  79.7 us (16%)
  matrix products  79 us (16%)
  between operations  13.5 us (3%)
  starting transfers between devices  5.6 us (1%)
    ppermute x2, waiting for transfers between devices, ring_gather(): lower.append(lax.ppermute(lower[-1] if lower else x, axis, pairs))  93.8 us
    slice x8, local copies, waits for them, and re-layouts, attend(): keyvals[..., :feature_width].reshape(block_count, -1, HEADS, head_width)  72.7 us
    concatenate x4, other arithmetic, attend(): keyvals = jnp.concatenate([own_blocks[:, None], picked], axis=1)  40.3 us
    gather x4, local copies, waits for them, and re-layouts, one_group(): picked = pool[layout_part]  40 us
    dot_general x4, matrix products, attend(): jnp.einsum('bhqk,bkhd->bqhd', rounded, value_heads, preferred_element_typ...  35.2 us
    slice x4, local copies, waits for them, and re-layouts, attend(): keyvals[..., feature_width:].reshape(block_count, -1, HEADS, head_width)  33.4 us
    ppermute x1, waiting for transfers between devices, ring_gather(): upper.append(lax.ppermute(upper[-1] if upper else x, axis, back))  31.2 us
    concatenate x1, other arithmetic, shards(): jnp.concatenate([sums[1].astype(jnp.bfloat16), keyvals, sums[2].astype(jn...  21.3 us
  transfers between devices with their start and end apart: 6, of which 3 were waited for; matrix products, arithmetic and copies ran while one was open for 65% of the time, Pallas kernels for 0%

profile of v1, /device:TPU:0, one launch (start us, length us, event | category | flops | bytes accessed | tf_op | source)
XLA Modules:
  0.0 494.5 jit_solution(3664862388874395987)
XLA Ops:
  6.5 3.1 collective-permute-start
  9.6 2.0 collective-permute-start.2
  11.6 35.5 %collective-permute-done = bf16[256,3072]{1,0:T(8,128)(2,1)S(1)} collective-permute-done((bf16[256,3072]{1,0:T(8,128)(2,1)}, bf16[256,3072]{1,0:T(8,128)(2,1)S(1)}, u32[]{:S(2)}, u32[]{:S(2)}) %collective-permute-start) | collective-permute-done | bytes 1572896 | tf_op jit(solution)/shard_map/ppermute | solution.py:25
  47.7 0.7 reshape.196
  48.4 31.2 %collective-permute-done.2 = bf16[256,3072]{1,0:T(8,128)(2,1)S(1)} collective-permute-done((bf16[256,3072]{1,0:T(8,128)(2,1)}, bf16[256,3072]{1,0:T(8,128)(2,1)S(1)}, u32[]{:S(2)}, u32[]{:S(2)}) %collective-permute-start.2) | collective-permute-done | bytes 1572896 | tf_op jit(solution)/shard_map/ppermute | solution.py:27
  79.6 58.3 %collective-permute-done.1 = bf16[256,3072]{1,0:T(8,128)(2,1)} collective-permute-done((bf16[256,3072]{1,0:T(8,128)(2,1)S(1)}, bf16[256,3072]{1,0:T(8,128)(2,1)}, u32[]{:S(2)}, u32[]{:S(2)}) %collective-permute-start.1) | collective-permute-done | bytes 1572896 | tf_op jit(solution)/shard_map/ppermute | solution.py:25
  137.9 5.2 %pad_maximum_fusion.2 = bf16[4,256,3072]{2,1,0:T(8,128)(2,1)} fusion(bf16[1,256,3072]{2,1,0:T(8,128)(2,1)S(1)} %bitcast.99, bf16[1,256,3072]{2,1,0:T(8,128)(2,1)} %bitcast.97, bf16[1,256,3072]{2,1,0:T(8,128)(2,1)S(1)} %bitcast.98, bf16[1,256,3072]{2,1,0:T(8,128)(2,1)} %bitcast.13), kind=kLoop, calls=%fused_computation.37 | loop fusion | flops 9437184 | bytes 12582912 | tf_op jit(solution)/shard_map/stack | solution.py:28
  143.2 6.5 %gather_fusion.1 = bf16[4,256,3072]{2,1,0:T(8,128)(2,1)} fusion(bf16[4,256,3072]{2,1,0:T(8,128)(2,1)} %pad_maximum_fusion.2, s32[1024]{0:T(1024)S(1)} %pad_clamp_fusion.1), kind=kCustom, calls=%fused_computation.1 | custom fusion | bytes 12582928 | tf_op jit(solution)/shard_map/gather | solution.py:30
  149.7 9.6 %convert_bitcast_fusion = bf16[1024,3072]{1,0:T(8,128)(2,1)S(1)} fusion(bf16[1024,1024]{1,0:T(8,128)(2,1)S(1)} %copy-done.3, bf16[1024,3072]{1,0:T(8,128)(2,1)} %bitcast.94), kind=kOutput, calls=%fused_computation.38 | convolution fusion | flops 6445596672 | bytes 14680064 | tf_op jit(solution)/shard_map/dot_general | solution.py:77
  159.4 5.0 %copy-done.2 = bf16[4,256,3072]{2,1,0:T(8,128)(2,1)S(1)} copy-done((bf16[4,256,3072]{2,1,0:T(8,128)(2,1)S(1)}, bf16[4,256,3072]{2,1,0:T(8,128)(2,1)}, u32[]{:S(2)}) %copy-start.2) | copy-done | bytes 6291480
  164.4 6.3 %convert_bitcast_fusion.1 = bf16[1024,2048]{1,0:T(8,128)(2,1)S(1)} fusion(bf16[1024,1024]{1,0:T(8,128)(2,1)} %collective-permute-done.4, bf16[1024,3072]{1,0:T(8,128)(2,1)S(1)} %bitcast.95), kind=kOutput, calls=%fused_computation.39 | convolution fusion | flops 4297064448 | bytes 10485760 | tf_op jit(solution)/shard_map/dot_general | solution.py:81
  170.8 6.5 %convert_bitcast_fusion.2 = bf16[1024,2048]{1,0:T(8,128)(2,1)S(1)} fusion(bf16[1024,1024]{1,0:T(8,128)(2,1)} %collective-permute-done.3, bf16[1024,3072]{1,0:T(8,128)(2,1)S(1)} %bitcast.96), kind=kOutput, calls=%fused_computation.40 | convolution fusion | flops 4297064448 | bytes 10485760 | tf_op jit(solution)/shard_map/dot_general | solution.py:81
  177.3 21.3 %pad_maximum_fusion.1 = bf16[3072,2048]{1,0:T(8,128)(2,1)} fusion(bf16[1024,2048]{1,0:T(8,128)(2,1)S(1)} %convert_bitcast_fusion.1, bf16[1024,2048]{1,0:T(8,128)(2,1)S(1)} %slice-done, bf16[1024,2048]{1,0:T(8,128)(2,1)S(1)} %convert_bitcast_fusion.2), kind=kLoop, calls=%fused_computation.36 | loop fusion | flops 37748736 | bytes 25165824 | tf_op jit(solution)/shard_map/concatenate | solution.py:87
  198.6 283.2 %while.12 = (s32[]{:T(128)}, bf16[4,256,1024]{2,1,0:T(8,128)(2,1)}, s32[4]{0:T(128)S(1)}, bf16[24,128,2048]{2,1,0:T(8,128)(2,1)}, s32[4,2,10]{2,1,0:T(2,128)}, /...) while((s32[]{:T(128)}, bf16[4,256,1024]{2,1,0:T(8,128)(2,1)}, ...), condition=%wide.region_3.4_spmd, body=%wide.region_0.3_spmd.sunk | while | flops 1514416896 | bytes 190909680 | solution.py:102
  198.6 0.6 dynamic_slice.53
  199.8 1.3 dynamic-slice_bitcast_fusion.4
  201.1 0.7 compare_select_fusion.5
  201.9 10.0 %gather_fusion = bf16[20,128,2048]{2,1,0:T(8,128)(2,1)} fusion(bf16[24,128,2048]{2,1,0:T(8,128)(2,1)} %get-tuple-element.200, s32[1024]{0:T(1024)S(1)} %pad_clamp_fusion.3), kind=kCustom, calls=%fused_computation.clone.1 | custom fusion | bytes 20971600 | tf_op jit(solution)/shard_map/while/body/eval_jaxpr/gather | solution.py:99
  211.9 10.1 %pad_maximum_fusion.4 = bf16[2,11,128,2048]{3,2,1,0:T(8,128)(2,1)} fusion(bf16[2,10,128,2048]{3,2,1,0:T(8,128)(2,1)} %bitcast.89, bf16[2,1,128,2048]{3,2,1,0:T(8,128)(2,1)S(1)} %dynamic-slice_bitcast_fusion.4), kind=kLoop, calls=%fused_computation.2.clone.1 | loop fusion | flops 5767168 | bytes 23068672 | tf_op jit(solution)/shard_map/while/body/eval_jaxpr/concatenate | solution.py:44
  222.0 9.9 %fusion.46 = (bf16[2,1408,1024]{2,1,0:T(8,128)(2,1)}, bf16[2,1408,1024]{2,1,0:T(8,128)(2,1)}) fusion(bf16[2,1408,2048]{2,1,0:T(8,128)(2,1)} %bitcast.87), kind=kLoop, calls=%fused_computation.51.clone.1 | loop fusion | bytes 23068672 | tf_op jit(solution)/shard_map/while/body/eval_jaxpr/slice | solution.py:46
  231.9 8.2 %copy.26 = bf16[2,1408,1024]{1,2,0:T(8,128)(2,1)} copy(bf16[2,1408,1024]{2,1,0:T(8,128)(2,1)} %get-tuple-element.170) | data formatting | bytes 11534336 | tf_op jit(solution)/shard_map/while/body/eval_jaxpr/slice | solution.py:46
  240.4 3.9 fusion.48
  244.3 4.2 copy-done
  248.5 2.4 fusion.49
  250.9 8.3 %copy.25 = bf16[2,1408,1024]{1,2,0:T(8,128)(2,1)} copy(bf16[2,1408,1024]{2,1,0:T(8,128)(2,1)} %get-tuple-element.169) | data formatting | bytes 11534336 | tf_op jit(solution)/shard_map/while/body/eval_jaxpr/slice | solution.py:47
  259.2 8.8 %divide_convert_fusion.2 = bf16[2,128,8,128]{1,3,2,0:T(8,128)(2,1)S(1)} fusion(bf16[2,1408,8,128]{1,3,2,0:T(8,128)(2,1)} %bitcast.91, f32[2,8,128,1408]{3,2,1,0:T(8,128)} %copy-done, f32[2,8,128]{2,1,0:T(8,128)S(1)} %get-tuple-element.172, pred[2,1408]{1,0:T(4,128)(4,1)S(1)} %broadcast_compare_fusion.2, f32[2,128,8]{1,2,0:T(8,128)S(1)} %bitcast.100), kind=kOutput, calls=%fused_computation.14.clone.1 | convolution fusion | flops 750256128 | bytes 17844992 | tf_op jit(solution)/shard_map/while/body/eval_jaxpr/bhqk,bkhd->bqhd/dot_general | solution.py:60
  268.6 0.8 constant_dynamic-update-slice_fusion.2
  270.6 1.3 dynamic-slice_bitcast_fusion.4
  271.9 0.7 compare_select_fusion.5
  272.7 10.0 %gather_fusion = bf16[20,128,2048]{2,1,0:T(8,128)(2,1)} fusion(bf16[24,128,2048]{2,1,0:T(8,128)(2,1)} %get-tuple-element.200, s32[1024]{0:T(1024)S(1)} %pad_clamp_fusion.3), kind=kCustom, calls=%fused_computation.clone.1 | custom fusion | bytes 20971600 | tf_op jit(solution)/shard_map/while/body/eval_jaxpr/gather | solution.py:99
  282.7 10.1 %pad_maximum_fusion.4 = bf16[2,11,128,2048]{3,2,1,0:T(8,128)(2,1)} fusion(bf16[2,10,128,2048]{3,2,1,0:T(8,128)(2,1)} %bitcast.89, bf16[2,1,128,2048]{3,2,1,0:T(8,128)(2,1)S(1)} %dynamic-slice_bitcast_fusion.4), kind=kLoop, calls=%fused_computation.2.clone.1 | loop fusion | flops 5767168 | bytes 23068672 | tf_op jit(solution)/shard_map/while/body/eval_jaxpr/concatenate | solution.py:44
  292.8 9.9 %fusion.46 = (bf16[2,1408,1024]{2,1,0:T(8,128)(2,1)}, bf16[2,1408,1024]{2,1,0:T(8,128)(2,1)}) fusion(bf16[2,1408,2048]{2,1,0:T(8,128)(2,1)} %bitcast.87), kind=kLoop, calls=%fused_computation.51.clone.1 | loop fusion | bytes 23068672 | tf_op jit(solution)/shard_map/while/body/eval_jaxpr/slice | solution.py:46
  302.7 8.2 %copy.26 = bf16[2,1408,1024]{1,2,0:T(8,128)(2,1)} copy(bf16[2,1408,1024]{2,1,0:T(8,128)(2,1)} %get-tuple-element.170) | data formatting | bytes 11534336 | tf_op jit(solution)/shard_map/while/body/eval_jaxpr/slice | solution.py:46
  311.2 3.9 fusion.48
  315.1 4.2 copy-done
  319.3 2.4 fusion.49
  321.7 8.3 %copy.25 = bf16[2,1408,1024]{1,2,0:T(8,128)(2,1)} copy(bf16[2,1408,1024]{2,1,0:T(8,128)(2,1)} %get-tuple-element.169) | data formatting | bytes 11534336 | tf_op jit(solution)/shard_map/while/body/eval_jaxpr/slice | solution.py:47
  330.0 8.8 %divide_convert_fusion.2 = bf16[2,128,8,128]{1,3,2,0:T(8,128)(2,1)S(1)} fusion(bf16[2,1408,8,128]{1,3,2,0:T(8,128)(2,1)} %bitcast.91, f32[2,8,128,1408]{3,2,1,0:T(8,128)} %copy-done, f32[2,8,128]{2,1,0:T(8,128)S(1)} %get-tuple-element.172, pred[2,1408]{1,0:T(4,128)(4,1)S(1)} %broadcast_compare_fusion.2, f32[2,128,8]{1,2,0:T(8,128)S(1)} %bitcast.100), kind=kOutput, calls=%fused_computation.14.clone.1 | convolution fusion | flops 750256128 | bytes 17844992 | tf_op jit(solution)/shard_map/while/body/eval_jaxpr/bhqk,bkhd->bqhd/dot_general | solution.py:60
  339.4 0.9 constant_dynamic-update-slice_fusion.2
  341.5 1.3 dynamic-slice_bitcast_fusion.4
  342.8 0.7 compare_select_fusion.5
  343.5 10.0 %gather_fusion = bf16[20,128,2048]{2,1,0:T(8,128)(2,1)} fusion(bf16[24,128,2048]{2,1,0:T(8,128)(2,1)} %get-tuple-element.200, s32[1024]{0:T(1024)S(1)} %pad_clamp_fusion.3), kind=kCustom, calls=%fused_computation.clone.1 | custom fusion | bytes 20971600 | tf_op jit(solution)/shard_map/while/body/eval_jaxpr/gather | solution.py:99
  353.5 10.1 %pad_maximum_fusion.4 = bf16[2,11,128,2048]{3,2,1,0:T(8,128)(2,1)} fusion(bf16[2,10,128,2048]{3,2,1,0:T(8,128)(2,1)} %bitcast.89, bf16[2,1,128,2048]{3,2,1,0:T(8,128)(2,1)S(1)} %dynamic-slice_bitcast_fusion.4), kind=kLoop, calls=%fused_computation.2.clone.1 | loop fusion | flops 5767168 | bytes 23068672 | tf_op jit(solution)/shard_map/while/body/eval_jaxpr/concatenate | solution.py:44
  363.6 9.9 %fusion.46 = (bf16[2,1408,1024]{2,1,0:T(8,128)(2,1)}, bf16[2,1408,1024]{2,1,0:T(8,128)(2,1)}) fusion(bf16[2,1408,2048]{2,1,0:T(8,128)(2,1)} %bitcast.87), kind=kLoop, calls=%fused_computation.51.clone.1 | loop fusion | bytes 23068672 | tf_op jit(solution)/shard_map/while/body/eval_jaxpr/slice | solution.py:46
  373.6 8.2 %copy.26 = bf16[2,1408,1024]{1,2,0:T(8,128)(2,1)} copy(bf16[2,1408,1024]{2,1,0:T(8,128)(2,1)} %get-tuple-element.170) | data formatting | bytes 11534336 | tf_op jit(solution)/shard_map/while/body/eval_jaxpr/slice | solution.py:46
  382.0 3.9 fusion.48
  385.9 4.2 copy-done
  390.1 2.4 fusion.49
  392.5 8.3 %copy.25 = bf16[2,1408,1024]{1,2,0:T(8,128)(2,1)} copy(bf16[2,1408,1024]{2,1,0:T(8,128)(2,1)} %get-tuple-element.169) | data formatting | bytes 11534336 | tf_op jit(solution)/shard_map/while/body/eval_jaxpr/slice | solution.py:47
  400.9 8.8 %divide_convert_fusion.2 = bf16[2,128,8,128]{1,3,2,0:T(8,128)(2,1)S(1)} fusion(bf16[2,1408,8,128]{1,3,2,0:T(8,128)(2,1)} %bitcast.91, f32[2,8,128,1408]{3,2,1,0:T(8,128)} %copy-done, f32[2,8,128]{2,1,0:T(8,128)S(1)} %get-tuple-element.172, pred[2,1408]{1,0:T(4,128)(4,1)S(1)} %broadcast_compare_fusion.2, f32[2,128,8]{1,2,0:T(8,128)S(1)} %bitcast.100), kind=kOutput, calls=%fused_computation.14.clone.1 | convolution fusion | flops 750256128 | bytes 17844992 | tf_op jit(solution)/shard_map/while/body/eval_jaxpr/bhqk,bkhd->bqhd/dot_general | solution.py:60
  410.2 0.8 constant_dynamic-update-slice_fusion.2
  412.2 1.3 dynamic-slice_bitcast_fusion.4
  413.5 0.7 compare_select_fusion.5
  414.3 10.0 %gather_fusion = bf16[20,128,2048]{2,1,0:T(8,128)(2,1)} fusion(bf16[24,128,2048]{2,1,0:T(8,128)(2,1)} %get-tuple-element.200, s32[1024]{0:T(1024)S(1)} %pad_clamp_fusion.3), kind=kCustom, calls=%fused_computation.clone.1 | custom fusion | bytes 20971600 | tf_op jit(solution)/shard_map/while/body/eval_jaxpr/gather | solution.py:99
  424.3 10.1 %pad_maximum_fusion.4 = bf16[2,11,128,2048]{3,2,1,0:T(8,128)(2,1)} fusion(bf16[2,10,128,2048]{3,2,1,0:T(8,128)(2,1)} %bitcast.89, bf16[2,1,128,2048]{3,2,1,0:T(8,128)(2,1)S(1)} %dynamic-slice_bitcast_fusion.4), kind=kLoop, calls=%fused_computation.2.clone.1 | loop fusion | flops 5767168 | bytes 23068672 | tf_op jit(solution)/shard_map/while/body/eval_jaxpr/concatenate | solution.py:44
  434.4 9.9 %fusion.46 = (bf16[2,1408,1024]{2,1,0:T(8,128)(2,1)}, bf16[2,1408,1024]{2,1,0:T(8,128)(2,1)}) fusion(bf16[2,1408,2048]{2,1,0:T(8,128)(2,1)} %bitcast.87), kind=kLoop, calls=%fused_computation.51.clone.1 | loop fusion | bytes 23068672 | tf_op jit(solution)/shard_map/while/body/eval_jaxpr/slice | solution.py:46
  444.4 8.2 %copy.26 = bf16[2,1408,1024]{1,2,0:T(8,128)(2,1)} copy(bf16[2,1408,1024]{2,1,0:T(8,128)(2,1)} %get-tuple-element.170) | data formatting | bytes 11534336 | tf_op jit(solution)/shard_map/while/body/eval_jaxpr/slice | solution.py:46
  452.8 3.9 fusion.48
  456.7 4.2 copy-done
  460.9 2.4 fusion.49
  463.3 8.3 %copy.25 = bf16[2,1408,1024]{1,2,0:T(8,128)(2,1)} copy(bf16[2,1408,1024]{2,1,0:T(8,128)(2,1)} %get-tuple-element.169) | data formatting | bytes 11534336 | tf_op jit(solution)/shard_map/while/body/eval_jaxpr/slice | solution.py:47
  471.6 8.8 %divide_convert_fusion.2 = bf16[2,128,8,128]{1,3,2,0:T(8,128)(2,1)S(1)} fusion(bf16[2,1408,8,128]{1,3,2,0:T(8,128)(2,1)} %bitcast.91, f32[2,8,128,1408]{3,2,1,0:T(8,128)} %copy-done, f32[2,8,128]{2,1,0:T(8,128)S(1)} %get-tuple-element.172, pred[2,1408]{1,0:T(4,128)(4,1)S(1)} %broadcast_compare_fusion.2, f32[2,128,8]{1,2,0:T(8,128)S(1)} %bitcast.100), kind=kOutput, calls=%fused_computation.14.clone.1 | convolution fusion | flops 750256128 | bytes 17844992 | tf_op jit(solution)/shard_map/while/body/eval_jaxpr/bhqk,bkhd->bqhd/dot_general | solution.py:60
  481.0 0.8 constant_dynamic-update-slice_fusion.2
  481.8 5.9 %convolution_convert_fusion = bf16[1024,1024]{1,0:T(8,128)(2,1)} fusion(bf16[1024,1024]{1,0:T(8,128)(2,1)} %bitcast.102, bf16[1024,1024]{1,0:T(8,128)(2,1)} %all-gather.2.cloned.1.call-done), kind=kOutput, calls=%fused_computation.43 | convolution fusion | flops 2148532224 | bytes 6291456 | tf_op jit(solution)/shard_map/dot_general | solution.py:112
  (64 shorter events, 5.7 us)
Async XLA Ops:
  6.5 475.3 %all-gather.2.cloned.1.call-start = ((), (), s32[]{:S(2)}) async-start(), calls=%async_computation | async-start | bytes 2621440 | tf_op jit(solution)/shard_map/all_gather | solution.py:114
  6.5 40.6 %collective-permute-start = (bf16[256,3072]{1,0:T(8,128)(2,1)}, bf16[256,3072]{1,0:T(8,128)(2,1)S(1)}, u32[]{:S(2)}, u32[]{:S(2)}) collective-permute-start(bf16[256,3072]{1,0:T(8,128)(2,1)} %param.8), channel_id=1, source_target_pairs={{0,1},{1,2},{2,3},{3,0},{4,5},{5,6},{6,7},{7,4},{8,9},{9,10},{10,1... | collective-permute-start | bytes 4718600 | tf_op jit(solution)/shard_map/ppermute | solution.py:25
  9.6 70.0 %collective-permute-start.2 = (bf16[256,3072]{1,0:T(8,128)(2,1)}, bf16[256,3072]{1,0:T(8,128)(2,1)S(1)}, u32[]{:S(2)}, u32[]{:S(2)}) collective-permute-start(bf16[256,3072]{1,0:T(8,128)(2,1)} %param.8), channel_id=1, source_target_pairs={{1,0},{2,1},{3,2},{0,3},{5,4},{6,5},{7,6},{4,7},{9,8},{10,9},{11,1... | collective-permute-start | bytes 4718600 | tf_op jit(solution)/shard_map/ppermute | solution.py:27
  47.1 90.8 %collective-permute-start.1 = (bf16[256,3072]{1,0:T(8,128)(2,1)S(1)}, bf16[256,3072]{1,0:T(8,128)(2,1)}, u32[]{:S(2)}, u32[]{:S(2)}) collective-permute-start(bf16[256,3072]{1,0:T(8,128)(2,1)S(1)} %collective-permute-done), channel_id=1, source_target_pairs={{0,1},{1,2},{2,3},{3,0},{4,5},{5,6},{6,7},{7,4},{8,9},{9,10},{10,1... | collective-permute-start | bytes 4718600 | tf_op jit(solution)/shard_map/ppermute | solution.py:25
  47.1 112.2 %collective-permute-start.4 = (bf16[1024,1024]{1,0:T(8,128)(2,1)}, bf16[1024,1024]{1,0:T(8,128)(2,1)}, u32[]{:S(2)}, u32[]{:S(2)}) collective-permute-start(bf16[1024,1024]{1,0:T(8,128)(2,1)} %param.7), channel_id=1, source_target_pairs={{0,28},{4,0},{8,4},{12,8},{16,12},{20,16},{24,20},{28,24},{1,29},{... | collective-permute-start | bytes 6291464 | tf_op jit(solution)/shard_map/ppermute | solution.py:37
  47.4 123.4 %collective-permute-start.3 = (bf16[1024,1024]{1,0:T(8,128)(2,1)}, bf16[1024,1024]{1,0:T(8,128)(2,1)}, u32[]{:S(2)}, u32[]{:S(2)}) collective-permute-start(bf16[1024,1024]{1,0:T(8,128)(2,1)} %param.7), channel_id=1, source_target_pairs={{0,4},{4,8},{8,12},{12,16},{16,20},{20,24},{24,28},{28,0},{1,5},{5... | collective-permute-start | bytes 6291464 | tf_op jit(solution)/shard_map/ppermute | solution.py:37
  143.2 6.5 %copy-start.3 = (bf16[1024,1024]{1,0:T(8,128)(2,1)S(1)}, bf16[1024,1024]{1,0:T(8,128)(2,1)}, u32[]{:S(2)}) copy-start(bf16[1024,1024]{1,0:T(8,128)(2,1)} %param.7) | copy-start | bytes 6291460
  159.3 11.4 %copy-start.1 = (bf16[1024,3072]{1,0:T(8,128)(2,1)}, bf16[1024,3072]{1,0:T(8,128)(2,1)S(1)}, u32[]{:S(2)}) copy-start(bf16[1024,3072]{1,0:T(8,128)(2,1)S(1)} %convert_bitcast_fusion) | copy-start | bytes 18874372
  159.3 5.1 %copy-start.2 = (bf16[4,256,3072]{2,1,0:T(8,128)(2,1)S(1)}, bf16[4,256,3072]{2,1,0:T(8,128)(2,1)}, u32[]{:S(2)}) copy-start(bf16[4,256,3072]{2,1,0:T(8,128)(2,1)} %gather_fusion.1) | copy-start | bytes 18874372
  170.7 6.5 %slice-start = ((bf16[1024,3072]{1,0:T(8,128)(2,1)}), bf16[1024,2048]{1,0:T(8,128)(2,1)S(1)}, s32[]{:S(2)}) async-start(bf16[1024,3072]{1,0:T(8,128)(2,1)} %copy-done.1), calls=%async_computation.1 | async-start | bytes 8388608 | tf_op jit(solution)/shard_map/slice | solution.py:86
  177.3 21.4 %slice-start.1 = ((bf16[1024,3072]{1,0:T(8,128)(2,1)}), bf16[1024,1024]{1,0:T(8,128)(2,1)S(1)}, s32[]{:S(2)}) async-start(bf16[1024,3072]{1,0:T(8,128)(2,1)} %copy-done.1), calls=%async_computation.2 | async-start | bytes 4194304 | tf_op jit(solution)/shard_map/slice | solution.py:85
  244.3 4.2 copy-start
  315.1 4.2 copy-start
  385.9 4.2 copy-start
  456.7 4.2 copy-start
Sparse Core Ops, SparseCore 0:
  47.8 100.0 all-gather.1
